TPU v7x, 32 devices: a whole 2x2x4 slice. The times are simulated.
32 devices in a mesh: sky: 8 (over z, x), tm: 4 (over y, core).
Axes of the slice: x: 2, y: 2, z: 4, core: 2. Of those that a mesh axis runs over, the one named last changes fastest.
Arguments:
- observed: float32 [4096, 128], P(('sky', 'tm')), may hold values from -12 to 12
- att_partials: bfloat16 [3, 4096, 128], P(None, ('sky', 'tm')), may hold values from -6 to 6
- src_partials: bfloat16 [5, 4096, 128], P(None, ('sky', 'tm')), may hold values from -6 to 6
- src_slot: int32 [4096], P(('sky', 'tm')), may hold values from 0 to 1023
- knot_block: int32 [4096], P(('sky', 'tm')), may hold values from 0 to 255, as said below
- live_count: int32 [32], P(('sky', 'tm')), may hold values from 32 to 128, as said below
- sources: float32 [5, 8192], P(None, 'sky'), may hold values from -6 to 6
- inverses: float32 [5, 5, 8192], P(None, None, 'sky')
- attitude: float32 [3, 4, 4096], P(None, 'tm', 'sky'), may hold values from -6 to 6
- band_coef: float32 [3, 3, 4, 4096], P(None, None, 'tm', 'sky'), may hold values from 0.5 to 4
- extra_diag: float32 [3, 4, 4096], P(None, 'tm', 'sky'), may hold values from 0.05 to 0.5
- band_offsets: int32 [3], replicated, may hold values from 1 to 16, as said below
Outputs:
- sources_out: float32 [5, 8192], P(None, 'sky')
- attitude_out: float32 [3, 4, 4096], P(None, 'tm', 'sky')
Inputs may be any that keep to these rules, and one draw needn't show every extreme that they name: On every device, the crossings name blocks of one holder (knot_block // 32) at most 32 times, and some holder exactly 32 times; dead crossings carry blocks too. `live_count`: some device uses all its crossings. `band_offsets`: Distinct; one of them is 16.
All inputs are finite; a program needn't handle non-finite values.
Results may differ from a plain program's by a relative error of at most 0.0003.
Values sent between devices are 32-bit elements; how exact they have to be, the bound alone decides.
A program may use at most 64 MiB of HBM per device.

v0:
```python
import jax
import jax.numpy as jnp
from jax import lax
from jax.sharding import PartitionSpec as P

ROWS = 128
BLOCK_KNOTS = 16
HW = 16
SWEEPS = 3
ITERS = 2


def padded_2(block, sides, width):
    for axis, dim in sides:
        count = lax.axis_size(axis)
        forward = [(i, i + 1) for i in range(count - 1)]
        forward.append((count - 1, 0))
        backward = [(target, source) for source, target in forward]
        low = lax.ppermute(
            lax.slice_in_dim(block, block.shape[dim] - width, None, axis=dim), axis, forward
        )
        high = lax.ppermute(lax.slice_in_dim(block, 0, width, axis=dim), axis, backward)
        block = jnp.concatenate([low, block, high], axis=dim)
    return block


def from_behind(value, axis, steps):
    count = lax.axis_size(axis)
    initial, last = (max(0, -steps), min(count, count - steps))
    return lax.ppermute(value, axis, [(source, source + steps) for source in range(initial, last)])


def spline_table():
    rows_pos = jnp.arange(ROWS, dtype=jnp.float32)
    moments = 1.5 + (BLOCK_KNOTS - 3) * (rows_pos + 0.5) / ROWS
    knot_pos = jnp.arange(BLOCK_KNOTS, dtype=jnp.float32)
    dist = jnp.abs(moments[:, None] - knot_pos[None, :])
    inner = 2.0 / 3.0 - dist * dist + 0.5 * dist * dist * dist
    rest = 2.0 - dist
    outer = rest * rest * rest / 6.0
    return jnp.where(dist < 1.0, inner, jnp.where(dist < 2.0, outer, 0.0))


def source_term(src_partials, values):
    total = jnp.zeros(src_partials.shape[1:], jnp.float32)
    for component in range(5):
        total = total + src_partials[component].astype(jnp.float32) * values[component][:, None]
    return total


def neighbour_sum(field, band_terms, band_offsets, base, length):
    total = jnp.zeros(band_terms.shape[1:], jnp.float32)
    for band_index in range(band_terms.shape[0]):
        offset = band_offsets[band_index]
        upper = lax.dynamic_slice_in_dim(field, base + offset, length, 1)
        lower = lax.dynamic_slice_in_dim(field, base - offset, length, 1)
        total = total + band_terms[band_index] * (upper + lower)
    return total


def extend(field, width):
    padded = padded_2(field, (("sky", 1),), width)
    inner_end = padded.shape[1] - width
    left_rim = padded[:, :width]
    right_rim = padded[:, inner_end:]
    from_before = from_behind(left_rim, "tm", 1)
    from_after = from_behind(right_rim, "tm", -1)
    position = lax.axis_index("sky")
    left_rim = jnp.where(position == 0, from_before, left_rim)
    right_rim = jnp.where(position == lax.axis_size("sky") - 1, from_after, right_rim)
    return jnp.concatenate([left_rim, padded[:, width:inner_end], right_rim], axis=1)


def per_device(
    observed,
    att_partials,
    src_partials,
    src_slot,
    knot_block,
    live_count,
    sources,
    inverses,
    attitude,
    band_coef,
    extra_diag,
    band_offsets,
):
    spline = spline_table()
    crossings_here = observed.shape[0]
    knots_here = attitude.shape[2]
    blocks_here = knots_here // BLOCK_KNOTS
    sky_count = lax.axis_size("sky")
    capacity = 2 * crossings_here // sky_count
    slots_total = sky_count * capacity
    live_rows = (jnp.arange(crossings_here, dtype=jnp.int32) < live_count[0]).astype(jnp.float32)[
        :, None
    ]
    band_terms = band_coef[:, :, 0, :]
    extra_terms = extra_diag[:, 0, :]
    diagonal = extra_terms + 2.0 * jnp.sum(band_terms, axis=0)
    knots_now = attitude[:, 0, :]
    sources_now = sources
    holder = knot_block // blocks_here
    local_block = knot_block % blocks_here
    matches = (holder[:, None] == jnp.arange(sky_count, dtype=jnp.int32)[None, :]).astype(jnp.int32)
    earlier = jnp.cumsum(matches, axis=0) - matches
    column = holder * capacity + jnp.sum(earlier * matches, axis=1)
    asked = jnp.full((slots_total,), blocks_here, jnp.int32).at[column].set(local_block)
    wanted = lax.all_to_all(asked, "sky", split_axis=0, concat_axis=0, tiled=True)
    for outer_step in range(ITERS):
        spare = jnp.zeros((3, 1, BLOCK_KNOTS), jnp.float32)
        own_blocks = jnp.concatenate(
            [knots_now.reshape(3, blocks_here, BLOCK_KNOTS), spare], axis=1
        )
        served = jnp.take(jnp.transpose(own_blocks, (0, 2, 1)), wanted, axis=2)
        arrived = lax.all_to_all(served, "sky", split_axis=2, concat_axis=2, tiled=True)
        fetched = jnp.transpose(jnp.take(arrived, column, axis=2), (0, 2, 1))
        att_term = jnp.zeros(observed.shape, jnp.float32)
        for axis_index in range(3):
            att_term = att_term + att_partials[axis_index].astype(jnp.float32) * jnp.dot(
                fetched[axis_index], spline.T, precision=lax.Precision.HIGHEST
            )
        src_values = jnp.take(sources_now, src_slot, axis=1)
        resid = (observed - source_term(src_partials, src_values) - att_term) * live_rows
        rhs = jnp.stack(
            [
                jnp.sum(src_partials[component].astype(jnp.float32) * resid, axis=1)
                for component in range(5)
            ]
        )
        local_normal = jnp.zeros(sources_now.shape, jnp.float32).at[:, src_slot].add(rhs)
        normal = lax.psum(local_normal, "tm")
        step = jnp.einsum("klm,lm->km", inverses, normal, precision=lax.Precision.HIGHEST)
        sources_now = sources_now + step
        resid = resid - live_rows * source_term(src_partials, jnp.take(step, src_slot, axis=1))
        grads = jnp.stack(
            [
                jnp.dot(
                    att_partials[axis_index].astype(jnp.float32) * resid,
                    spline,
                    precision=lax.Precision.HIGHEST,
                )
                for axis_index in range(3)
            ]
        )
        outgoing = (
            jnp.zeros((3, BLOCK_KNOTS, slots_total), jnp.float32)
            .at[:, :, column]
            .set(jnp.transpose(grads, (0, 2, 1)))
        )
        returned = lax.all_to_all(outgoing, "sky", split_axis=2, concat_axis=2, tiled=True)
        summed = (
            jnp.zeros((3, BLOCK_KNOTS, blocks_here + 1), jnp.float32).at[:, :, wanted].add(returned)
        )
        knot_grad = jnp.transpose(summed[:, :, :blocks_here], (0, 2, 1)).reshape(3, knots_here)
        delta = knot_grad / diagonal
        for sweep_index in range(SWEEPS - 1):
            widened = extend(delta, HW)
            delta = (
                knot_grad + neighbour_sum(widened, band_terms, band_offsets, HW, knots_here)
            ) / diagonal
        knots_now = knots_now + delta
    return (sources_now, knots_now[:, None, :])


def solution(mesh):
    placed = (
        P(("sky", "tm"), None),
        P(None, ("sky", "tm"), None),
        P(None, ("sky", "tm"), None),
        P(("sky", "tm")),
        P(("sky", "tm")),
        P(("sky", "tm")),
        P(None, "sky"),
        P(None, None, "sky"),
        P(None, "tm", "sky"),
        P(None, None, "tm", "sky"),
        P(None, "tm", "sky"),
        P(),
    )
    return jax.shard_map(
        per_device,
        mesh=mesh,
        in_specs=placed,
        out_specs=(P(None, "sky"), P(None, "tm", "sky")),
        check_vma=False,
    )
```

profile of v0, /device:TPU:0, one launch (start us, length us, event | category | flops | bytes accessed | tf_op | source)
XLA Modules:
  0.0 228.7 jit_solution(7839276913477497021)
XLA Ops:
  3.4 7.3 %all-to-all-start = ((s32[8,32,1]{1,2,0:T(1,128)}), s32[8,32,1]{1,2,0:T(1,128)S(1)}, u32[]{:S(2)}, u32[]{:S(2)}) async-start(s32[8,32,1]{1,2,0:T(1,128)} %bitcast.8), calls=%async_computation | async-start | bytes 8192 | tf_op jit(solution)/shard_map/all_to_all | solution.py:109
  11.4 1.4 fusion.182
  28.3 3.6 %copy.86 = f32[5,5,1024]{0,1,2:T(8,128)} copy(f32[5,5,1024]{2,1,0:T(8,128)} %param.25) | data formatting | bytes 204800 | tf_op args[7]
  35.6 6.0 %all-to-all-start.1 = ((f32[8,1,1536]{2,1,0:T(1,128)}), f32[8,1,1536]{2,1,0:T(1,128)S(1)}, u32[]{:S(2)}, u32[]{:S(2)}) async-start(f32[8,1,1536]{2,1,0:T(1,128)} %reshape.339), calls=%async_computation.1 | async-start | bytes 98304 | tf_op jit(solution)/shard_map/all_to_all | solution.py:116
  41.7 6.7 %all-to-all-done.1 = f32[8,1,1536]{2,1,0:T(1,128)S(1)} async-done(((f32[8,1,1536]{2,1,0:T(1,128)}), f32[8,1,1536]{2,1,0:T(1,128)S(1)}, u32[]{:S(2)}, u32[]{:S(2)}) %all-to-all-start.1) | async-done | bytes 49184 | tf_op jit(solution)/shard_map/all_to_all | solution.py:116
  53.4 16.1 %psum.14 = f32[5,1024]{0,1:T(8,128)S(1)} all-reduce(f32[5,1024]{0,1:T(8,128)S(1)} %scatter_custom_fusion.1), channel_id=1, replica_groups=mesh['sky'=8,'tm'=4] {'tm'}, use_global_device_ids=true, to_apply=%region_9.13 | all-reduce | flops 5120 | bytes 40960 | tf_op jit(solution)/shard_map/psum | solution.py:132
  69.5 8.5 %fusion.185 = f32[1024,1,5]{2,1,0:T(1,128)S(1)} fusion(f32[5,1024,1]{0,2,1:T(1,128)S(1)} %bitcast.304, f32[5,5,1024]{0,1,2:T(8,128)} %copy.86), kind=kOutput, calls=%fused_computation.312 | convolution fusion | flops 307200 | bytes 143360 | tf_op jit(solution)/shard_map/klm,lm->km/dot_general | solution.py:133
  81.1 4.3 %scatter_fusion = f32[3,16,256]{1,0,2:T(4,128)S(1)} fusion(f32[3,16,256]{1,0,2:T(4,128)S(1)} %broadcast.97.clone, s32[128]{0:T(128)S(1)} %get-tuple-element.44, f32[128,3,16]{2,1,0:T(4,128)S(1)} %copy.74), kind=kCustom, calls=%fused_computation.10 | custom fusion | bytes 74240 | tf_op jit(solution)/shard_map/scatter | solution.py:149
  86.4 3.5 %all-to-all-start.2 = ((f32[8,1,1536]{2,1,0:T(1,128)}), f32[8,1,1536]{2,1,0:T(1,128)S(1)}, u32[]{:S(2)}, u32[]{:S(2)}) async-start(f32[8,1,1536]{2,1,0:T(1,128)} %reshape.341), calls=%async_computation.2 | async-start | bytes 98304 | tf_op jit(solution)/shard_map/all_to_all | solution.py:151
  89.9 6.7 %all-to-all-done.2 = f32[8,1,1536]{2,1,0:T(1,128)S(1)} async-done(((f32[8,1,1536]{2,1,0:T(1,128)}), f32[8,1,1536]{2,1,0:T(1,128)S(1)}, u32[]{:S(2)}, u32[]{:S(2)}) %all-to-all-start.2) | async-done | bytes 49184 | tf_op jit(solution)/shard_map/all_to_all | solution.py:151
  97.9 8.8 %scatter_fusion.1 = f32[3,16,33]{1,0,2:T(4,128)S(1)} fusion(f32[3,16,33]{1,0,2:T(4,128)S(1)} %broadcast.94.clone, s32[256]{0:T(256)S(1)} %bitcast.316, f32[256,3,16]{2,1,0:T(4,128)S(1)} %bitcast_bitcast_fusion.1), kind=kCustom, calls=%fused_computation.11 | custom fusion | flops 12288 | bytes 148480 | tf_op jit(solution)/shard_map/scatter-add | solution.py:153
  107.3 4.3 %collective-permute-start.2 = (f32[3,16]{1,0:T(4,128)S(1)}, f32[3,16]{1,0:T(4,128)S(1)}, u32[]{:S(2)}, u32[]{:S(2)}) collective-permute-start(f32[3,16]{1,0:T(4,128)S(1)} %get-tuple-element.69), channel_id=1, source_target_pairs={{4,0},{8,4},{12,8},{16,12},{20,16},{24,20},{28,24},{0,28},{5,1},{9... | collective-permute-start | bytes 584 | tf_op jit(solution)/shard_map/ppermute | solution.py:22
  111.6 1.6 collective-permute-done
  115.8 3.4 %collective-permute-done.3 = f32[3,16]{1,0:T(4,128)S(1)} collective-permute-done((f32[3,16]{1,0:T(4,128)S(1)}, f32[3,16]{1,0:T(4,128)S(1)}, u32[]{:S(2)}, u32[]{:S(2)}) %collective-permute-start.3) | collective-permute-done | bytes 224 | tf_op jit(solution)/shard_map/ppermute | solution.py:30
  119.5 4.7 %collective-permute-start.6 = (f32[3,16]{1,0:T(4,128)S(1)}, f32[3,16]{1,0:T(4,128)S(1)}, u32[]{:S(2)}, u32[]{:S(2)}) collective-permute-start(f32[3,16]{1,0:T(4,128)S(1)} %get-tuple-element.67), channel_id=1, source_target_pairs={{4,0},{8,4},{12,8},{16,12},{20,16},{24,20},{28,24},{0,28},{5,1},{9... | collective-permute-start | bytes 584 | tf_op jit(solution)/shard_map/ppermute | solution.py:22
  124.2 1.6 collective-permute-done.4
  125.7 3.1 %collective-permute-start.5 = (f32[3,16]{1,0:T(4,128)S(1)}, f32[3,16]{1,0:T(4,128)S(1)}, u32[]{:S(2)}, u32[]{:S(2)}) collective-permute-start(f32[3,16]{1,0:T(4,128)S(1)} %collective-permute-done.4), channel_id=1, source_target_pairs={{0,1},{1,2},{2,3},{4,5},{5,6},{6,7},{8,9},{9,10},{10,11},{12,13},{... | collective-permute-start | bytes 584 | tf_op jit(solution)/shard_map/ppermute | solution.py:30
  130.2 2.4 %collective-permute-done.7 = f32[3,16]{1,0:T(4,128)S(1)} collective-permute-done((f32[3,16]{1,0:T(4,128)S(1)}, f32[3,16]{1,0:T(4,128)S(1)}, u32[]{:S(2)}, u32[]{:S(2)}) %collective-permute-start.7) | collective-permute-done | bytes 224 | tf_op jit(solution)/shard_map/ppermute | solution.py:30
  135.3 3.3 %all-to-all-start.3 = ((f32[8,1,1536]{2,1,0:T(1,128)}), f32[8,1,1536]{2,1,0:T(1,128)S(1)}, u32[]{:S(2)}, u32[]{:S(2)}) async-start(f32[8,1,1536]{2,1,0:T(1,128)} %reshape.343), calls=%async_computation.3 | async-start | bytes 98304 | tf_op jit(solution)/shard_map/all_to_all | solution.py:116
  138.9 6.5 %all-to-all-done.3 = f32[8,1,1536]{2,1,0:T(1,128)S(1)} async-done(((f32[8,1,1536]{2,1,0:T(1,128)}), f32[8,1,1536]{2,1,0:T(1,128)S(1)}, u32[]{:S(2)}, u32[]{:S(2)}) %all-to-all-start.3) | async-done | bytes 49184 | tf_op jit(solution)/shard_map/all_to_all | solution.py:116
  149.8 16.9 %psum.15 = f32[5,1024]{0,1:T(8,128)S(1)} all-reduce(f32[5,1024]{0,1:T(8,128)S(1)} %scatter_custom_fusion.4), channel_id=1, replica_groups=mesh['sky'=8,'tm'=4] {'tm'}, use_global_device_ids=true, to_apply=%region_19.23 | all-reduce | flops 5120 | bytes 40960 | tf_op jit(solution)/shard_map/psum | solution.py:132
  166.7 8.5 %fusion.186 = f32[1024,1,5]{2,1,0:T(1,128)S(1)} fusion(f32[5,1024,1]{0,2,1:T(1,128)S(1)} %bitcast.303, f32[5,5,1024]{0,1,2:T(8,128)} %copy.86), kind=kOutput, calls=%fused_computation.313 | convolution fusion | flops 307200 | bytes 143360 | tf_op jit(solution)/shard_map/klm,lm->km/dot_general | solution.py:133
  177.6 4.3 %scatter_fusion.2 = f32[3,16,256]{1,0,2:T(4,128)S(1)} fusion(f32[3,16,256]{1,0,2:T(4,128)S(1)} %broadcast.97, s32[128]{0:T(128)S(1)} %get-tuple-element.44, f32[128,3,16]{2,1,0:T(4,128)S(1)} %copy.81), kind=kCustom, calls=%fused_computation.13 | custom fusion | bytes 74240 | tf_op jit(solution)/shard_map/scatter | solution.py:149
  182.3 9.2 %all_to_all.35 = f32[8,1,1536]{2,1,0:T(1,128)S(1)} all-to-all(f32[8,1,1536]{2,1,0:T(1,128)S(1)} %reshape.345), channel_id=1, replica_groups=mesh['sky'=8,'tm'=4] {'sky'}, dimensions={0} | all-to-all | bytes 98304 | tf_op jit(solution)/shard_map/all_to_all | solution.py:151
  192.7 8.8 %scatter_fusion.3 = f32[3,16,33]{1,0,2:T(4,128)S(1)} fusion(f32[3,16,33]{1,0,2:T(4,128)S(1)} %broadcast.94, s32[256]{0:T(256)S(1)} %bitcast.317, f32[256,3,16]{2,1,0:T(4,128)S(1)} %bitcast_bitcast_fusion), kind=kCustom, calls=%fused_computation.14 | custom fusion | flops 12288 | bytes 148480 | tf_op jit(solution)/shard_map/scatter-add | solution.py:153
  202.0 4.3 %collective-permute-start.10 = (f32[3,16]{1,0:T(4,128)S(1)}, f32[3,16]{1,0:T(4,128)S(1)}, u32[]{:S(2)}, u32[]{:S(2)}) collective-permute-start(f32[3,16]{1,0:T(4,128)S(1)} %get-tuple-element.65), channel_id=1, source_target_pairs={{4,0},{8,4},{12,8},{16,12},{20,16},{24,20},{28,24},{0,28},{5,1},{9... | collective-permute-start | bytes 584 | tf_op jit(solution)/shard_map/ppermute | solution.py:22
  206.4 1.6 collective-permute-done.8
  210.6 3.1 %collective-permute-done.11 = f32[3,16]{1,0:T(4,128)S(1)} collective-permute-done((f32[3,16]{1,0:T(4,128)S(1)}, f32[3,16]{1,0:T(4,128)S(1)}, u32[]{:S(2)}, u32[]{:S(2)}) %collective-permute-start.11) | collective-permute-done | bytes 224 | tf_op jit(solution)/shard_map/ppermute | solution.py:30
  214.0 4.8 %collective-permute-start.14 = (f32[3,16]{1,0:T(4,128)S(1)}, f32[3,16]{1,0:T(4,128)S(1)}, u32[]{:S(2)}, u32[]{:S(2)}) collective-permute-start(f32[3,16]{1,0:T(4,128)S(1)} %get-tuple-element.63), channel_id=1, source_target_pairs={{4,0},{8,4},{12,8},{16,12},{20,16},{24,20},{28,24},{0,28},{5,1},{9... | collective-permute-start | bytes 584 | tf_op jit(solution)/shard_map/ppermute | solution.py:22
  218.8 1.4 collective-permute-done.12
  220.2 3.1 %collective-permute-start.13 = (f32[3,16]{1,0:T(4,128)S(1)}, f32[3,16]{1,0:T(4,128)S(1)}, u32[]{:S(2)}, u32[]{:S(2)}) collective-permute-start(f32[3,16]{1,0:T(4,128)S(1)} %collective-permute-done.12), channel_id=1, source_target_pairs={{0,1},{1,2},{2,3},{4,5},{5,6},{6,7},{8,9},{9,10},{10,11},{12,13},{... | collective-permute-start | bytes 584 | tf_op jit(solution)/shard_map/ppermute | solution.py:30
  225.4 2.4 %collective-permute-done.15 = f32[3,16]{1,0:T(4,128)S(1)} collective-permute-done((f32[3,16]{1,0:T(4,128)S(1)}, f32[3,16]{1,0:T(4,128)S(1)}, u32[]{:S(2)}, u32[]{:S(2)}) %collective-permute-start.15) | collective-permute-done | bytes 224 | tf_op jit(solution)/shard_map/ppermute | solution.py:30
  (162 shorter events, 46.5 us)
Async XLA Ops:
  0.6 31.3 %copy-start = (f32[3,3,1,512]{3,2,1,0:T(1,128)S(1)}, f32[3,3,1,512]{3,2,1,0:T(1,128)}, u32[]{:S(2)}) copy-start(f32[3,3,1,512]{3,2,1,0:T(1,128)} %param.27) | copy-start | bytes 55300
  3.4 28.5 %all-to-all-start = ((s32[8,32,1]{1,2,0:T(1,128)}), s32[8,32,1]{1,2,0:T(1,128)S(1)}, u32[]{:S(2)}, u32[]{:S(2)}) async-start(s32[8,32,1]{1,2,0:T(1,128)} %bitcast.8), calls=%async_computation | async-start | bytes 8192 | tf_op jit(solution)/shard_map/all_to_all | solution.py:109
  35.6 12.8 %all-to-all-start.1 = ((f32[8,1,1536]{2,1,0:T(1,128)}), f32[8,1,1536]{2,1,0:T(1,128)S(1)}, u32[]{:S(2)}, u32[]{:S(2)}) async-start(f32[8,1,1536]{2,1,0:T(1,128)} %reshape.339), calls=%async_computation.1 | async-start | bytes 98304 | tf_op jit(solution)/shard_map/all_to_all | solution.py:116
  78.0 28.7 %copy-start.2 = (f32[3,1,512]{2,1,0:T(1,128)S(1)}, f32[3,1,512]{2,1,0:T(1,128)}, u32[]{:S(2)}) copy-start(f32[3,1,512]{2,1,0:T(1,128)} %param.28) | copy-start | bytes 18436
  78.1 54.6 %copy-start.1 = (f32[3,1,512]{2,1,0:T(1,128)S(1)}, f32[3,1,512]{2,1,0:T(1,128)}, u32[]{:S(2)}) copy-start(f32[3,1,512]{2,1,0:T(1,128)} %param.26) | copy-start | bytes 18436
  86.4 10.3 %all-to-all-start.2 = ((f32[8,1,1536]{2,1,0:T(1,128)}), f32[8,1,1536]{2,1,0:T(1,128)S(1)}, u32[]{:S(2)}, u32[]{:S(2)}) async-start(f32[8,1,1536]{2,1,0:T(1,128)} %reshape.341), calls=%async_computation.2 | async-start | bytes 98304 | tf_op jit(solution)/shard_map/all_to_all | solution.py:151
  106.9 6.3 %collective-permute-start = (f32[3,16]{1,0:T(4,128)S(1)}, f32[3,16]{1,0:T(4,128)S(1)}, u32[]{:S(2)}, u32[]{:S(2)}) collective-permute-start(f32[3,16]{1,0:T(4,128)S(1)} %get-tuple-element.68), channel_id=1, source_target_pairs={{0,4},{4,8},{8,12},{12,16},{16,20},{20,24},{24,28},{28,0},{1,5},{5... | collective-permute-start | bytes 584 | tf_op jit(solution)/shard_map/ppermute | solution.py:19
  107.3 7.2 %collective-permute-start.2 = (f32[3,16]{1,0:T(4,128)S(1)}, f32[3,16]{1,0:T(4,128)S(1)}, u32[]{:S(2)}, u32[]{:S(2)}) collective-permute-start(f32[3,16]{1,0:T(4,128)S(1)} %get-tuple-element.69), channel_id=1, source_target_pairs={{4,0},{8,4},{12,8},{16,12},{20,16},{24,20},{28,24},{0,28},{5,1},{9... | collective-permute-start | bytes 584 | tf_op jit(solution)/shard_map/ppermute | solution.py:22
  113.2 2.6 %collective-permute-start.1 = (f32[3,16]{1,0:T(4,128)S(1)}, f32[3,16]{1,0:T(4,128)S(1)}, u32[]{:S(2)}, u32[]{:S(2)}) collective-permute-start(f32[3,16]{1,0:T(4,128)S(1)} %collective-permute-done), channel_id=1, source_target_pairs={{0,1},{1,2},{2,3},{4,5},{5,6},{6,7},{8,9},{9,10},{10,11},{12,13},{... | collective-permute-start | bytes 584 | tf_op jit(solution)/shard_map/ppermute | solution.py:30
  114.5 4.7 %collective-permute-start.3 = (f32[3,16]{1,0:T(4,128)S(1)}, f32[3,16]{1,0:T(4,128)S(1)}, u32[]{:S(2)}, u32[]{:S(2)}) collective-permute-start(f32[3,16]{1,0:T(4,128)S(1)} %collective-permute-done.2), channel_id=1, source_target_pairs={{1,0},{2,1},{3,2},{5,4},{6,5},{7,6},{9,8},{10,9},{11,10},{13,12},{... | collective-permute-start | bytes 584 | tf_op jit(solution)/shard_map/ppermute | solution.py:30
  119.5 6.3 %collective-permute-start.4 = (f32[3,16]{1,0:T(4,128)S(1)}, f32[3,16]{1,0:T(4,128)S(1)}, u32[]{:S(2)}, u32[]{:S(2)}) collective-permute-start(f32[3,16]{1,0:T(4,128)S(1)} %get-tuple-element.66), channel_id=1, source_target_pairs={{0,4},{4,8},{8,12},{12,16},{16,20},{20,24},{24,28},{28,0},{1,5},{5... | collective-permute-start | bytes 584 | tf_op jit(solution)/shard_map/ppermute | solution.py:19
  119.5 9.4 %collective-permute-start.6 = (f32[3,16]{1,0:T(4,128)S(1)}, f32[3,16]{1,0:T(4,128)S(1)}, u32[]{:S(2)}, u32[]{:S(2)}) collective-permute-start(f32[3,16]{1,0:T(4,128)S(1)} %get-tuple-element.67), channel_id=1, source_target_pairs={{4,0},{8,4},{12,8},{16,12},{20,16},{24,20},{28,24},{0,28},{5,1},{9... | collective-permute-start | bytes 584 | tf_op jit(solution)/shard_map/ppermute | solution.py:22
  125.7 4.4 %collective-permute-start.5 = (f32[3,16]{1,0:T(4,128)S(1)}, f32[3,16]{1,0:T(4,128)S(1)}, u32[]{:S(2)}, u32[]{:S(2)}) collective-permute-start(f32[3,16]{1,0:T(4,128)S(1)} %collective-permute-done.4), channel_id=1, source_target_pairs={{0,1},{1,2},{2,3},{4,5},{5,6},{6,7},{8,9},{9,10},{10,11},{12,13},{... | collective-permute-start | bytes 584 | tf_op jit(solution)/shard_map/ppermute | solution.py:30
  128.8 3.8 %collective-permute-start.7 = (f32[3,16]{1,0:T(4,128)S(1)}, f32[3,16]{1,0:T(4,128)S(1)}, u32[]{:S(2)}, u32[]{:S(2)}) collective-permute-start(f32[3,16]{1,0:T(4,128)S(1)} %collective-permute-done.6), channel_id=1, source_target_pairs={{1,0},{2,1},{3,2},{5,4},{6,5},{7,6},{9,8},{10,9},{11,10},{13,12},{... | collective-permute-start | bytes 584 | tf_op jit(solution)/shard_map/ppermute | solution.py:30
  135.3 10.1 %all-to-all-start.3 = ((f32[8,1,1536]{2,1,0:T(1,128)}), f32[8,1,1536]{2,1,0:T(1,128)S(1)}, u32[]{:S(2)}, u32[]{:S(2)}) async-start(f32[8,1,1536]{2,1,0:T(1,128)} %reshape.343), calls=%async_computation.3 | async-start | bytes 98304 | tf_op jit(solution)/shard_map/all_to_all | solution.py:116
  201.7 6.3 %collective-permute-start.8 = (f32[3,16]{1,0:T(4,128)S(1)}, f32[3,16]{1,0:T(4,128)S(1)}, u32[]{:S(2)}, u32[]{:S(2)}) collective-permute-start(f32[3,16]{1,0:T(4,128)S(1)} %get-tuple-element.64), channel_id=1, source_target_pairs={{0,4},{4,8},{8,12},{12,16},{16,20},{20,24},{24,28},{28,0},{1,5},{5... | collective-permute-start | bytes 584 | tf_op jit(solution)/shard_map/ppermute | solution.py:19
  202.0 7.2 %collective-permute-start.10 = (f32[3,16]{1,0:T(4,128)S(1)}, f32[3,16]{1,0:T(4,128)S(1)}, u32[]{:S(2)}, u32[]{:S(2)}) collective-permute-start(f32[3,16]{1,0:T(4,128)S(1)} %get-tuple-element.65), channel_id=1, source_target_pairs={{4,0},{8,4},{12,8},{16,12},{20,16},{24,20},{28,24},{0,28},{5,1},{9... | collective-permute-start | bytes 584 | tf_op jit(solution)/shard_map/ppermute | solution.py:22
  207.9 2.6 %collective-permute-start.9 = (f32[3,16]{1,0:T(4,128)S(1)}, f32[3,16]{1,0:T(4,128)S(1)}, u32[]{:S(2)}, u32[]{:S(2)}) collective-permute-start(f32[3,16]{1,0:T(4,128)S(1)} %collective-permute-done.8), channel_id=1, source_target_pairs={{0,1},{1,2},{2,3},{4,5},{5,6},{6,7},{8,9},{9,10},{10,11},{12,13},{... | collective-permute-start | bytes 584 | tf_op jit(solution)/shard_map/ppermute | solution.py:30
  209.2 4.4 %collective-permute-start.11 = (f32[3,16]{1,0:T(4,128)S(1)}, f32[3,16]{1,0:T(4,128)S(1)}, u32[]{:S(2)}, u32[]{:S(2)}) collective-permute-start(f32[3,16]{1,0:T(4,128)S(1)} %collective-permute-done.10), channel_id=1, source_target_pairs={{1,0},{2,1},{3,2},{5,4},{6,5},{7,6},{9,8},{10,9},{11,10},{13,12},{... | collective-permute-start | bytes 584 | tf_op jit(solution)/shard_map/ppermute | solution.py:30
  213.9 6.3 %collective-permute-start.12 = (f32[3,16]{1,0:T(4,128)S(1)}, f32[3,16]{1,0:T(4,128)S(1)}, u32[]{:S(2)}, u32[]{:S(2)}) collective-permute-start(f32[3,16]{1,0:T(4,128)S(1)} %get-tuple-element.62), channel_id=1, source_target_pairs={{0,4},{4,8},{8,12},{12,16},{16,20},{20,24},{24,28},{28,0},{1,5},{5... | collective-permute-start | bytes 584 | tf_op jit(solution)/shard_map/ppermute | solution.py:19
  214.0 10.1 %collective-permute-start.14 = (f32[3,16]{1,0:T(4,128)S(1)}, f32[3,16]{1,0:T(4,128)S(1)}, u32[]{:S(2)}, u32[]{:S(2)}) collective-permute-start(f32[3,16]{1,0:T(4,128)S(1)} %get-tuple-element.63), channel_id=1, source_target_pairs={{4,0},{8,4},{12,8},{16,12},{20,16},{24,20},{28,24},{0,28},{5,1},{9... | collective-permute-start | bytes 584 | tf_op jit(solution)/shard_map/ppermute | solution.py:22
  220.2 5.2 %collective-permute-start.13 = (f32[3,16]{1,0:T(4,128)S(1)}, f32[3,16]{1,0:T(4,128)S(1)}, u32[]{:S(2)}, u32[]{:S(2)}) collective-permute-start(f32[3,16]{1,0:T(4,128)S(1)} %collective-permute-done.12), channel_id=1, source_target_pairs={{0,1},{1,2},{2,3},{4,5},{5,6},{6,7},{8,9},{9,10},{10,11},{12,13},{... | collective-permute-start | bytes 584 | tf_op jit(solution)/shard_map/ppermute | solution.py:30
  224.1 3.7 %collective-permute-start.15 = (f32[3,16]{1,0:T(4,128)S(1)}, f32[3,16]{1,0:T(4,128)S(1)}, u32[]{:S(2)}, u32[]{:S(2)}) collective-permute-start(f32[3,16]{1,0:T(4,128)S(1)} %collective-permute-done.14), channel_id=1, source_target_pairs={{1,0},{2,1},{3,2},{5,4},{6,5},{7,6},{9,8},{10,9},{11,10},{13,12},{... | collective-permute-start | bytes 584 | tf_op jit(solution)/shard_map/ppermute | solution.py:30
where the time goes:
time: 232 us; the launch traced here: 229 us
  starting transfers between devices  53 us (23%)
  blocking collectives  42.2 us (18%)
  waiting for transfers between devices  37.4 us (16%)
  local copies, waits for them, and re-layouts  37 us (16%)
  other arithmetic  28.4 us (12%)
  matrix products  20.9 us (9%)
  between operations  9.85 us (4%)
    psum x2, blocking collectives, per_device(): normal = lax.psum(local_normal, 'tm')  33 us
    ppermute x4, starting transfers between devices, padded_2(): lax.ppermute(lax.slice_in_dim(block, 0, width, axis=dim), axis, backward)  18.2 us
    scatter-add x2, other arithmetic, per_device(): jnp.zeros((3, BLOCK_KNOTS, blocks_here + 1), jnp.float32).at[:, :, wanted]  17.5 us
    dot_general x2, matrix products, per_device(): jnp.einsum('klm,lm->km', inverses, normal, precision=lax.Precision.HIGHEST)  17.1 us
    ppermute x8, starting transfers between devices, from_behind(): lax.ppermute(value, axis, [(source, source + steps) for source in range(i...  13.9 us
    all_to_all x2, waiting for transfers between devices, per_device(): lax.all_to_all(served, 'sky', split_axis=2, concat_axis=2, tiled=True)  13.2 us
    unnamed x27, local copies, waits for them, and re-layouts  12.5 us
    ppermute x8, waiting for transfers between devices, from_behind(): lax.ppermute(value, axis, [(source, source + steps) for source in range(i...  11.4 us
  transfers between devices with their start and end apart: 20, of which 11 were waited for; matrix products, arithmetic and copies ran while one was open for 6% of the time, Pallas kernels for 0%

commit v1 on v0

v1 whole, which is shorter than its diff:
```python
import functools

import jax
import jax.numpy as jnp
from jax import lax
from jax.experimental import pallas as pl
from jax.experimental.pallas import tpu as pltpu
from jax.sharding import PartitionSpec as P

BLOCK_KNOTS = 16
SWEEPS = 3
ITERS = 2
NPAR = 5
NAX = 3
LANES = 128
HALO = 8
MESH = pl.DeviceIdType.MESH
F32 = jnp.float32
BF16 = jnp.bfloat16

NN = (((1,), (0,)), ((), ()))
NT = (((1,), (1,)), ((), ()))


def iota(shape, dim):
    return lax.broadcasted_iota(jnp.int32, shape, dim)


def onehot(mask):
    return jnp.where(mask, 1.0, 0.0).astype(BF16)


def parts(x):
    high = x.astype(BF16)
    rest = x - high.astype(F32)
    mid = rest.astype(BF16)
    low = (rest - mid.astype(F32)).astype(BF16)
    return high, mid, low


def mm(a, b, dims):
    return lax.dot_general(a, b, dims, preferred_element_type=F32)


def pick_left(hot, x, dims=NN):
    high, mid, low = parts(x)
    return mm(hot, high, dims) + (mm(hot, mid, dims) + mm(hot, low, dims))


def pick_right(x, hot, dims=NN):
    high, mid, low = parts(x)
    return mm(high, hot, dims) + (mm(mid, hot, dims) + mm(low, hot, dims))


def full_dot(x, y_parts):
    total = None
    x_parts = parts(x)
    for i in (2, 1, 0):
        for j in range(3 - i):
            term = mm(x_parts[i], y_parts[j], NN)
            total = term if total is None else total + term
    return total


def spline_at(row, knot, rows):
    moment = 1.5 + (BLOCK_KNOTS - 3) * (row.astype(F32) + 0.5) / rows
    dist = jnp.abs(moment - knot.astype(F32))
    inner = 2.0 / 3.0 - dist * dist + 0.5 * dist * dist * dist
    rest = 2.0 - dist
    outer = rest * rest * rest / 6.0
    return jnp.where(dist < 1.0, inner, jnp.where(dist < 2.0, outer, 0.0))


def to_blocks(rows, nblocks, fold):
    length = rows[0].shape[1]
    own = (iota((nblocks, length), 1) >> 4) == iota((nblocks, length), 0)
    stacked = jnp.concatenate([jnp.where(own, row, 0.0) for row in rows], axis=0)
    spread = pick_right(stacked, fold)
    lane = iota((nblocks, LANES), 1) >> 4
    out = jnp.zeros((nblocks, LANES), F32)
    for a in range(NAX):
        out = jnp.where(lane == a, spread[a * nblocks : (a + 1) * nblocks], out)
    return out


def kernel(
    n_sky,
    n_tm,
    observed,
    att_partials,
    src_partials,
    src_slot,
    knot_block,
    live_count,
    sources,
    inverses,
    attitude,
    band_coef,
    extra_diag,
    band_offsets,
    sources_out,
    attitude_out,
    knots_all,
    rhs_all,
    grad_mine,
    rim_mine,
    grad_all,
    rim_low,
    rim_high,
    edge_mine,
    edge_near,
    knots_send,
    knots_recv,
    rhs_send,
    rhs_recv,
    grad_send,
    grad_recv,
    rim_send,
    low_recv,
    high_recv,
    edge_send,
    edge_recv,
):
    s = lax.axis_index("sky")
    t = lax.axis_index("tm")
    cross, rows = observed.shape
    knots_here = attitude.shape[2]
    blocks = knots_here // BLOCK_KNOTS
    half = blocks // 2
    span = blocks + 2 * HALO
    span2 = span // 2
    n_blocks = n_sky * blocks
    n_src = sources.shape[1]
    n_band = band_coef.shape[0]

    first_t, last_t = t == 0, t == n_tm - 1
    at_low, at_high = s == 0, s == n_sky - 1
    from_low = jnp.logical_and(at_low, t > 0)
    from_high = jnp.logical_and(at_high, t < n_tm - 1)
    has_left = jnp.logical_not(jnp.logical_and(at_low, first_t))
    has_right = jnp.logical_not(jnp.logical_and(at_high, last_t))
    right = (jnp.where(at_high, 0, s + 1), jnp.where(at_high, jnp.minimum(t + 1, n_tm - 1), t))
    left = (jnp.where(at_low, n_sky - 1, s - 1), jnp.where(at_low, jnp.maximum(t - 1, 0), t))

    barrier = pltpu.get_barrier_semaphore()
    for i in range(1, n_sky):
        pl.semaphore_signal(
            barrier, inc=1, device_id=(lax.rem(s + i, n_sky), t), device_id_type=MESH
        )
    for i in range(1, n_tm):
        pl.semaphore_signal(
            barrier, inc=1, device_id=(s, lax.rem(t + i, n_tm)), device_id_type=MESH
        )

    @pl.when(from_low)
    def _():
        for i in range(n_sky):
            pl.semaphore_signal(barrier, inc=1, device_id=(i, jnp.maximum(t - 1, 0)), device_id_type=MESH)

    @pl.when(from_high)
    def _():
        for i in range(n_sky):
            pl.semaphore_signal(barrier, inc=1, device_id=(i, jnp.minimum(t + 1, n_tm - 1)), device_id_type=MESH)

    def knots_copy(it, i):
        return pltpu.make_async_remote_copy(
            src_ref=knots_all.at[it, s],
            dst_ref=knots_all.at[it, s],
            send_sem=knots_send.at[it, i],
            recv_sem=knots_recv.at[it, i],
            device_id=(lax.rem(s + i, n_sky), t),
            device_id_type=MESH,
        )

    def rhs_copy(it, i):
        return pltpu.make_async_remote_copy(
            src_ref=rhs_all.at[it, t],
            dst_ref=rhs_all.at[it, t],
            send_sem=rhs_send.at[it, i],
            recv_sem=rhs_recv.at[it, i],
            device_id=(s, lax.rem(t + i, n_tm)),
            device_id_type=MESH,
        )

    def grad_copy(it, i):
        to = lax.rem(s + i, n_sky)
        return pltpu.make_async_remote_copy(
            src_ref=grad_mine.at[it, to],
            dst_ref=grad_all.at[it, s],
            send_sem=grad_send.at[it, i],
            recv_sem=grad_recv.at[it, i],
            device_id=(to, t),
            device_id_type=MESH,
        )

    def low_copy(it, sender):
        return pltpu.make_async_remote_copy(
            src_ref=rim_mine.at[it, 0],
            dst_ref=rim_low.at[it, sender],
            send_sem=rim_send.at[it, 0],
            recv_sem=low_recv.at[it, sender],
            device_id=(0, jnp.minimum(t + 1, n_tm - 1)),
            device_id_type=MESH,
        )

    def high_copy(it, sender):
        return pltpu.make_async_remote_copy(
            src_ref=rim_mine.at[it, 1],
            dst_ref=rim_high.at[it, sender],
            send_sem=rim_send.at[it, 1],
            recv_sem=high_recv.at[it, sender],
            device_id=(n_sky - 1, jnp.maximum(t - 1, 0)),
            device_id_type=MESH,
        )

    def edge_copy(side):
        return pltpu.make_async_remote_copy(
            src_ref=edge_mine.at[side],
            dst_ref=edge_near.at[side],
            send_sem=edge_send.at[side],
            recv_sem=edge_recv.at[side],
            device_id=right if side == 0 else left,
            device_id_type=MESH,
        )

    def pack(own):
        return own[:half] + pltpu.roll(own[half:], LANES // 2, 1)

    fold_own = onehot(
        (iota((knots_here, LANES), 0) & 15) == (iota((knots_here, LANES), 1) & 15)
    )
    knots_own = to_blocks([attitude[a] for a in range(NAX)], blocks, fold_own)
    knots_all[0, s] = pack(knots_own)
    lines = [band_coef[b, a] for b in range(n_band) for a in range(NAX)]
    lines = lines + [extra_diag[a] for a in range(NAX)]
    spare = [jnp.zeros((16 - len(lines), LANES), F32)]
    edge_mine[0] = jnp.concatenate([x[:, knots_here - LANES :] for x in lines] + spare, axis=0)
    edge_mine[1] = jnp.concatenate([x[:, :LANES] for x in lines] + spare, axis=0)

    need = (n_sky - 1) + (n_tm - 1) + (t < n_tm - 1).astype(jnp.int32) + (t > 0).astype(jnp.int32)
    pl.semaphore_wait(barrier, need)

    @pl.when(jnp.logical_not(from_low))
    def _():
        rim_low[...] = jnp.zeros(rim_low.shape, F32)

    @pl.when(jnp.logical_not(from_high))
    def _():
        rim_high[...] = jnp.zeros(rim_high.shape, F32)

    for i in range(1, n_sky):
        knots_copy(0, i).start()

    @pl.when(has_right)
    def _():
        edge_copy(0).start()

    @pl.when(has_left)
    def _():
        edge_copy(1).start()

    slot_row = src_slot[...].astype(F32)
    block_row = knot_block[...].astype(F32)
    slot_col = jnp.transpose(jnp.broadcast_to(slot_row, (LANES, cross)))
    block_col = jnp.transpose(jnp.broadcast_to(block_row, (LANES, cross)))
    holder_col = jnp.floor((block_col + 0.5) / blocks)
    local_col = block_col - holder_col * blocks
    upper_col = jnp.where(local_col >= half, 1.0, 0.0)
    place_col = holder_col * half + local_col - upper_col * half

    width = n_sky * half
    knot_hot = onehot(iota((cross, width), 1).astype(F32) == place_col[:, :1])
    lane_upper = jnp.where(iota((cross, LANES), 1) >= LANES // 2, 1.0, 0.0)
    half_mask = lane_upper == upper_col

    gap_rows = jnp.zeros((8 - NPAR, n_src), F32)
    src_list = [x for q in range(NPAR) for x in (inverses[q], gap_rows)]
    src_rows = jnp.concatenate(src_list + [sources[...], gap_rows], axis=0)
    n_rows = src_rows.shape[0]
    src_hot = onehot(iota((cross, n_src), 1).astype(F32) == slot_col[:, :1])
    gathered = pick_left(src_hot, src_rows, NT)

    wide = NPAR * rows
    sel_row = iota((n_rows, wide), 0)
    sel_col = iota((n_rows, wide), 1) // rows
    step_sel = onehot((sel_row >> 3) == sel_col)
    value_sel = onehot(sel_row - NPAR * 8 == sel_col)

    def source_term(spread):
        total = jnp.zeros((cross, rows), F32)
        for p in range(NPAR):
            total = total + src_partials[p].astype(F32) * spread[:, p * rows : (p + 1) * rows]
        return total

    base = observed[...] - source_term(pick_right(gathered, value_sel))
    live = iota((cross, rows), 0) < live_count[0]

    shape = (LANES, NAX * rows)
    c, d = iota(shape, 0) & 63, iota(shape, 1)
    fits = jnp.logical_and((c >> 4) == d // rows, c < NAX * BLOCK_KNOTS)
    look = parts(jnp.where(fits, spline_at(d % rows, c & 15, rows), 0.0))
    shape = (NAX * rows, LANES)
    c, d = iota(shape, 1) & 63, iota(shape, 0)
    fits = jnp.logical_and((c >> 4) == d // rows, c < NAX * BLOCK_KNOTS)
    back = parts(jnp.where(fits, spline_at(d % rows, c & 15, rows), 0.0))

    sum_rows = onehot(iota((16, wide), 0) == iota((16, wide), 1) // rows)

    total_rows = n_sky * span2 + 2 * HALO
    m = iota((total_rows, cross), 0)
    low_target = m - HALO
    high_target = m - HALO + span2
    for h in range(1, n_sky):
        low_target = low_target + jnp.where(m >= h * span2, blocks - span2, 0)
        high_target = high_target + jnp.where(m >= h * span2, blocks - span2, 0)
    extra_row = m - n_sky * span2
    low_target = jnp.where(extra_row >= 0, n_blocks - HALO + extra_row, low_target)
    low_target = jnp.where(extra_row >= HALO, -1, low_target)
    high_target = jnp.where(extra_row >= 0, extra_row - HALO, high_target)
    window_hot = jnp.concatenate(
        [onehot(low_target == knot_block[...]), onehot(high_target == knot_block[...])], axis=1
    )
    lane_low = iota((cross, LANES), 1) < LANES // 2

    shape = (3 * LANES, n_band * LANES)
    c, d = iota(shape, 0), iota(shape, 1)
    from_knot = (c & 15) + ((c >> 7) - 1) * BLOCK_KNOTS
    gap = jnp.abs(from_knot - (d & 15))
    same = jnp.logical_and((c & 127) >> 4 == (d & 127) >> 4, (d & 127) < NAX * BLOCK_KNOTS)
    offset = jnp.zeros(shape, jnp.int32)
    for b in range(n_band):
        offset = jnp.where((d >> 7) == b, band_offsets[b], offset)
    shift_hot = onehot(jnp.logical_and(same, gap == offset))

    for i in range(1, n_sky):
        knots_copy(0, i).wait_recv()

    rhs_total = None
    for it in range(ITERS):
        fetched = pick_left(knot_hot, knots_all[it].reshape(width, LANES))
        fetched = jnp.where(half_mask, fetched, 0.0)
        seen = full_dot(fetched, look)
        att_term = jnp.zeros((cross, rows), F32)
        for a in range(NAX):
            att_term = att_term + att_partials[a].astype(F32) * seen[:, a * rows : (a + 1) * rows]
        resid = jnp.where(live, base - att_term, 0.0)
        weighted = jnp.concatenate(
            [src_partials[p].astype(F32) * resid for p in range(NPAR)], axis=1
        )
        rhs = pick_left(sum_rows, weighted, NT)[:8]
        row = iota((8, cross), 0)
        rhs_all[it, t] = jnp.where(row == NPAR, slot_row, rhs)
        for i in range(1, n_tm):
            rhs_copy(it, i).start()

        if it == 0:
            @pl.when(has_left)
            def _():
                edge_copy(0).wait_recv()

            @pl.when(has_right)
            def _():
                edge_copy(1).wait_recv()

            row = iota((16, LANES), 0)
            blank = jnp.where(
                jnp.logical_and(row >= n_band * NAX, row < (n_band + 1) * NAX), 1.0, 0.0
            )

            @pl.when(jnp.logical_not(has_left))
            def _():
                edge_near[0] = blank

            @pl.when(jnp.logical_not(has_right))
            def _():
                edge_near[1] = blank

            length = knots_here + 2 * LANES
            fold = onehot((iota((length, LANES), 0) & 15) == (iota((length, LANES), 1) & 15))

            near_low, near_high = edge_near[0], edge_near[1]

            def window(at, line):
                return jnp.concatenate(
                    [near_low[at : at + 1], line, near_high[at : at + 1]], axis=1
                )

            bands = [
                to_blocks([window(b * NAX + a, band_coef[b, a]) for a in range(NAX)], span, fold)
                for b in range(n_band)
            ]
            extra = to_blocks(
                [window(n_band * NAX + a, extra_diag[a]) for a in range(NAX)], span, fold
            )
            band_sum = bands[0]
            for b in range(1, n_band):
                band_sum = band_sum + bands[b]
            valid = iota((span, LANES), 1) < NAX * BLOCK_KNOTS
            inv_diag = 1.0 / jnp.where(valid, extra + 2.0 * band_sum, 1.0)

        for i in range(1, n_tm):
            rhs_copy(it, i).wait_recv()
        got = [rhs_all[it, i] for i in range(n_tm)]
        if it == 0:
            same_source = jnp.concatenate(
                [onehot(slot_col == g[NPAR : NPAR + 1]) for g in got], axis=1
            )
            slots_all = jnp.concatenate([g[NPAR : NPAR + 1] for g in got], axis=1)
        rhs_now = jnp.concatenate(got, axis=1)
        rhs_now = jnp.where(iota(rhs_now.shape, 0) < NPAR, rhs_now, 0.0)
        rhs_total = rhs_now if rhs_total is None else rhs_total + rhs_now
        tiled = jnp.concatenate([rhs_now] * NPAR + [jnp.zeros_like(rhs_now)], axis=0)
        normal = pick_left(same_source, tiled, NT)
        moved = source_term(pick_right(gathered * normal, step_sel))
        base = base - moved
        resid = resid - jnp.where(live, moved, 0.0)

        pulled = jnp.concatenate(
            [att_partials[a].astype(F32) * resid for a in range(NAX)], axis=1
        )
        grads = full_dot(pulled, back)
        both = jnp.concatenate(
            [jnp.where(lane_low, grads, 0.0), jnp.where(lane_low, 0.0, grads)], axis=0
        )
        windows = pick_left(window_hot, both)
        grad_mine[it] = windows[: n_sky * span2].reshape(n_sky, span2, LANES)
        rim_mine[it] = windows[n_sky * span2 :].reshape(2, HALO, LANES)
        for i in range(1, n_sky):
            grad_copy(it, i).start()

        @pl.when(t < n_tm - 1)
        def _():
            low_copy(it, s).start()

        @pl.when(t > 0)
        def _():
            high_copy(it, s).start()

        grad_all[it, s] = grad_mine[it, s]

        if it == ITERS - 1:
            full_hot = onehot(
                iota((n_src, n_tm * cross), 0).astype(F32) == slots_all
            )
            padded = jnp.concatenate([rhs_total, jnp.zeros_like(rhs_total)], axis=0)
            normal_all = pick_right(padded, full_hot, NT)[:NPAR]
            steps = [
                jnp.sum(inverses[q] * normal_all, axis=0, keepdims=True) for q in range(NPAR)
            ]
            sources_out[...] = sources[...] + jnp.concatenate(steps, axis=0)

        for i in range(1, n_sky):
            grad_copy(it, i).wait_recv()

        @pl.when(from_low)
        def _():
            for i in range(n_sky):
                low_copy(it, i).wait_recv()

        @pl.when(from_high)
        def _():
            for i in range(n_sky):
                high_copy(it, i).wait_recv()

        packed = grad_all[it, 0]
        for i in range(1, n_sky):
            packed = packed + grad_all[it, i]
        low, high = rim_low[it, 0], rim_high[it, 0]
        for i in range(1, n_sky):
            low, high = low + rim_low[it, i], high + rim_high[it, i]
        packed = jnp.concatenate(
            [packed[:HALO] + low, packed[HALO : span2 - HALO], packed[span2 - HALO :] + high],
            axis=0,
        )
        grad = jnp.concatenate([packed, pltpu.roll(packed, LANES // 2, 1)], axis=0)
        grad = jnp.where(valid, grad, 0.0)
        delta = grad * inv_diag
        for sweep in range(SWEEPS - 1):
            near = jnp.concatenate(
                [pltpu.roll(delta, 1, 0), delta, pltpu.roll(delta, span - 1, 0)], axis=1
            )
            sums = pick_right(near, shift_hot)
            total = grad
            for b in range(n_band):
                total = total + bands[b] * sums[:, b * LANES : (b + 1) * LANES]
            delta = total * inv_diag
        knots_own = knots_own + delta[HALO : HALO + blocks]
        if it < ITERS - 1:
            knots_all[it + 1, s] = pack(knots_own)
            for i in range(1, n_sky):
                knots_copy(it + 1, i).start()
            for i in range(1, n_sky):
                knots_copy(it + 1, i).wait_recv()

    shape = (LANES, knots_here)
    c, d = iota(shape, 0), iota(shape, 1)
    own = (iota((blocks, knots_here), 1) >> 4) == iota((blocks, knots_here), 0)
    for a in range(NAX):
        unfold = onehot(jnp.logical_and((c >> 4) == a, (c & 15) == (d & 15)))
        line = jnp.where(own, pick_right(knots_own, unfold), 0.0)
        attitude_out[a] = jnp.sum(line, axis=0, keepdims=True)

    for it in range(ITERS):
        for i in range(1, n_sky):
            knots_copy(it, i).wait_send()
            grad_copy(it, i).wait_send()
        for i in range(1, n_tm):
            rhs_copy(it, i).wait_send()

        @pl.when(t < n_tm - 1)
        def _():
            low_copy(it, s).wait_send()

        @pl.when(t > 0)
        def _():
            high_copy(it, s).wait_send()

    @pl.when(has_right)
    def _():
        edge_copy(0).wait_send()

    @pl.when(has_left)
    def _():
        edge_copy(1).wait_send()


def per_device(
    observed,
    att_partials,
    src_partials,
    src_slot,
    knot_block,
    live_count,
    sources,
    inverses,
    attitude,
    band_coef,
    extra_diag,
    band_offsets,
):
    n_sky, n_tm = lax.axis_size("sky"), lax.axis_size("tm")
    blocks = attitude.shape[2] // BLOCK_KNOTS
    span2 = (blocks + 2 * HALO) // 2
    vmem = pl.BlockSpec(memory_space=pltpu.VMEM)
    smem = pl.BlockSpec(memory_space=pltpu.SMEM)
    dma = pltpu.SemaphoreType.DMA
    return pl.pallas_call(
        functools.partial(kernel, n_sky, n_tm),
        out_shape=(
            jax.ShapeDtypeStruct(sources.shape, F32),
            jax.ShapeDtypeStruct(attitude.shape, F32),
        ),
        in_specs=[vmem] * 5 + [smem] + [vmem] * 5 + [smem],
        out_specs=(vmem, vmem),
        scratch_shapes=[
            pltpu.VMEM((ITERS, n_sky, blocks // 2, LANES), F32),
            pltpu.VMEM((ITERS, n_tm, 8, src_slot.shape[0]), F32),
            pltpu.VMEM((ITERS, n_sky, span2, LANES), F32),
            pltpu.VMEM((ITERS, 2, HALO, LANES), F32),
            pltpu.VMEM((ITERS, n_sky, span2, LANES), F32),
            pltpu.VMEM((ITERS, n_sky, HALO, LANES), F32),
            pltpu.VMEM((ITERS, n_sky, HALO, LANES), F32),
            pltpu.VMEM((2, 16, LANES), F32),
            pltpu.VMEM((2, 16, LANES), F32),
            dma((ITERS, n_sky)),
            dma((ITERS, n_sky)),
            dma((ITERS, n_tm)),
            dma((ITERS, n_tm)),
            dma((ITERS, n_sky)),
            dma((ITERS, n_sky)),
            dma((ITERS, 2)),
            dma((ITERS, n_sky)),
            dma((ITERS, n_sky)),
            dma((2,)),
            dma((2,)),
        ],
        compiler_params=pltpu.CompilerParams(collective_id=0, has_side_effects=True),
    )(
        observed,
        att_partials,
        src_partials,
        src_slot[None, :],
        knot_block[None, :],
        live_count,
        sources,
        inverses,
        attitude,
        band_coef,
        extra_diag,
        band_offsets,
    )


def solution(mesh):
    placed = (
        P(("sky", "tm"), None),
        P(None, ("sky", "tm"), None),
        P(None, ("sky", "tm"), None),
        P(("sky", "tm")),
        P(("sky", "tm")),
        P(("sky", "tm")),
        P(None, "sky"),
        P(None, None, "sky"),
        P(None, "tm", "sky"),
        P(None, None, "tm", "sky"),
        P(None, "tm", "sky"),
        P(),
    )
    return jax.shard_map(
        per_device,
        mesh=mesh,
        in_specs=placed,
        out_specs=(P(None, "sky"), P(None, "tm", "sky")),
        check_vma=False,
    )
```

time: 232 us -> 43 us (0.19); the launches traced: 229 us -> 42.6 us
  starting transfers between devices: 53 us -> 0 us
  blocking collectives: 42.2 us -> 0 us
  Pallas kernels: 0 us -> 39.3 us
  waiting for transfers between devices: 37.4 us -> 0 us
  local copies, waits for them, and re-layouts: 37 us -> 1.98 us
  other arithmetic: 28.4 us -> 0 us
  matrix products: 20.9 us -> 0 us
  between operations: 9.85 us -> 1.3 us
    pallas_call x0 -> x1, Pallas kernels: none -> 39.3 us  [per_device(): pl.pallas_call(functools.partial(kernel, n_sky, n_tm), out_shape=(jax.Sha...]
    psum x2 -> x0, blocking collectives: 33 us -> none  [per_device(): normal = lax.psum(local_normal, 'tm')]
    ppermute x16 -> x0, starting transfers between devices: 32.8 us -> none  [the longest x4 18.2 us: padded_2(): lax.ppermute(lax.slice_in_dim(block, 0, width, axis=dim), axis, backward)]
    dot_general x14 -> x0, matrix products: 20.9 us -> none  [the longest x2 17.1 us: per_device(): jnp.einsum('klm,lm->km', inverses, normal, precision=lax.Precision.HIGHEST)]
    all_to_all x4 -> x0, starting transfers between devices: 20.1 us -> none  [the longest x2 9.34 us: per_device(): lax.all_to_all(served, 'sky', split_axis=2, concat_axis=2, tiled=True)]
    all_to_all x4 -> x0, waiting for transfers between devices: 19.9 us -> none  [the longest x2 13.2 us: per_device(): lax.all_to_all(served, 'sky', split_axis=2, concat_axis=2, tiled=True)]
    scatter-add x4 -> x0, other arithmetic: 19.8 us -> none  [the longest x2 17.5 us: per_device(): jnp.zeros((3, BLOCK_KNOTS, blocks_here + 1), jnp.float32).at[:, :, wanted]]
    ppermute x16 -> x0, waiting for transfers between devices: 17.5 us -> none  [the longest x8 11.4 us: from_behind(): lax.ppermute(value, axis, [(source, source + steps) for source in range(i...]
  transfers between devices with their start and end apart: 20 -> 0, of which waited for: 11 -> 0; matrix products, arithmetic and copies ran while one was open for 6% -> 0% of each run, Pallas kernels for 0% -> 0%
where the time goes in v1:
time: 43 us; the launch traced here: 42.6 us
  Pallas kernels  39.3 us (91%)
  local copies, waits for them, and re-layouts  1.98 us (5%)
  between operations  1.3 us (3%)
    pallas_call x1, Pallas kernels, per_device(): pl.pallas_call(functools.partial(kernel, n_sky, n_tm), out_shape=(jax.Sha...  39.3 us
    unnamed x4, local copies, waits for them, and re-layouts  1.98 us

profile of v1, /device:TPU:0, one launch (start us, length us, event | category | flops | bytes accessed | tf_op | source)
XLA Modules:
  0.0 42.6 jit_solution(6556079769024903533)
XLA Ops:
  1.3 39.3 %shard_map.131 = (f32[5,1024]{1,0:T(8,128)}, f32[3,1,512]{2,1,0:T(1,128)}) custom-call(f32[128,128]{1,0:T(8,128)} %observed.1, bf16[3,128,128]{2,1,0:T(8,128)(2,1)} %att_partials.1, bf16[5,128,128]{2,1,0:T(8,128)(2,1)} %src_partials.1, s32[1,128]{1,0:T(1,128)} %bitcast.2, s32[1,128]{1,0:T(1,128)} %bitcast.3, s32[1]{0:T(128)S(6)} %copy.16.live_count, ...), custom_call_target="tpu_custom_call" | custom-call | tf_op jit(solution)/shard_map/pallas_call | solution.py:547
  40.6 0.0 copy-start
  40.6 1.4 %copy.17 = f32[5,1024]{1,0:T(8,128)} copy(f32[5,1024]{1,0:T(8,128)} %get-tuple-element.4) | data formatting | bytes 40960
  42.0 0.0 copy-done
  42.0 0.6 %copy.18 = f32[3,1,512]{2,1,0:T(1,128)} copy(f32[3,1,512]{2,1,0:T(1,128)S(1)} %copy-done) | data formatting | bytes 12288
Async XLA Ops:
  40.6 1.4 %copy-start = (f32[3,1,512]{2,1,0:T(1,128)S(1)}, f32[3,1,512]{2,1,0:T(1,128)}, u32[]{:S(2)}) copy-start(f32[3,1,512]{2,1,0:T(1,128)} %get-tuple-element.5) | copy-start | bytes 18436

commit v2 on v1

--- a/solution.py
+++ b/solution.py
@@ -32,10 +32,7 @@
 
 def parts(x):
     high = x.astype(BF16)
-    rest = x - high.astype(F32)
-    mid = rest.astype(BF16)
-    low = (rest - mid.astype(F32)).astype(BF16)
-    return high, mid, low
+    return high, (x - high.astype(F32)).astype(BF16)
 
 
 def mm(a, b, dims):
@@ -43,23 +40,18 @@
 
 
 def pick_left(hot, x, dims=NN):
-    high, mid, low = parts(x)
-    return mm(hot, high, dims) + (mm(hot, mid, dims) + mm(hot, low, dims))
+    high, low = parts(x)
+    return mm(hot, high, dims) + mm(hot, low, dims)
 
 
 def pick_right(x, hot, dims=NN):
-    high, mid, low = parts(x)
-    return mm(high, hot, dims) + (mm(mid, hot, dims) + mm(low, hot, dims))
+    high, low = parts(x)
+    return mm(high, hot, dims) + mm(low, hot, dims)
 
 
 def full_dot(x, y_parts):
-    total = None
-    x_parts = parts(x)
-    for i in (2, 1, 0):
-        for j in range(3 - i):
-            term = mm(x_parts[i], y_parts[j], NN)
-            total = term if total is None else total + term
-    return total
+    high, low = parts(x)
+    return mm(high, y_parts[0], NN) + (mm(high, y_parts[1], NN) + mm(low, y_parts[0], NN))
 
 
 def spline_at(row, knot, rows):
@@ -230,6 +222,7 @@
         (iota((knots_here, LANES), 0) & 15) == (iota((knots_here, LANES), 1) & 15)
     )
     knots_own = to_blocks([attitude[a] for a in range(NAX)], blocks, fold_own)
+    knots_moved = jnp.zeros((blocks, LANES), F32)
     knots_all[0, s] = pack(knots_own)
     lines = [band_coef[b, a] for b in range(n_band) for a in range(NAX)]
     lines = lines + [extra_diag[a] for a in range(NAX)]
@@ -305,6 +298,18 @@
     back = parts(jnp.where(fits, spline_at(d % rows, c & 15, rows), 0.0))
 
     sum_rows = onehot(iota((16, wide), 0) == iota((16, wide), 1) // rows)
+
+    att = [att_partials[a].astype(F32) for a in range(NAX)]
+    cross_terms = []
+    for q in range(NPAR):
+        param = src_partials[q].astype(F32)
+        cross_terms.append(full_dot(jnp.concatenate([x * param for x in att], axis=1), back))
+
+    def against_params(value):
+        return [src_partials[p].astype(F32) * value for p in range(NPAR)]
+
+    on_base = against_params(base)
+    live_knots = iota((cross, LANES), 0) < live_count[0]
 
     total_rows = n_sky * span2 + 2 * HALO
     m = iota((total_rows, cross), 0)
@@ -339,19 +344,25 @@
     for it in range(ITERS):
         fetched = pick_left(knot_hot, knots_all[it].reshape(width, LANES))
         fetched = jnp.where(half_mask, fetched, 0.0)
-        seen = full_dot(fetched, look)
-        att_term = jnp.zeros((cross, rows), F32)
-        for a in range(NAX):
-            att_term = att_term + att_partials[a].astype(F32) * seen[:, a * rows : (a + 1) * rows]
-        resid = jnp.where(live, base - att_term, 0.0)
         weighted = jnp.concatenate(
-            [src_partials[p].astype(F32) * resid for p in range(NPAR)], axis=1
+            [
+                jnp.where(live, on_base[p] - fetched * cross_terms[p], 0.0)
+                for p in range(NPAR)
+            ],
+            axis=1,
         )
         rhs = pick_left(sum_rows, weighted, NT)[:8]
         row = iota((8, cross), 0)
         rhs_all[it, t] = jnp.where(row == NPAR, slot_row, rhs)
         for i in range(1, n_tm):
             rhs_copy(it, i).start()
+
+        seen = full_dot(fetched, look)
+        att_term = jnp.zeros((cross, rows), F32)
+        for a in range(NAX):
+            att_term = att_term + att[a] * seen[:, a * rows : (a + 1) * rows]
+        resid = jnp.where(live, base - att_term, 0.0)
+        grads_before = full_dot(jnp.concatenate([x * resid for x in att], axis=1), back)
 
         if it == 0:
             @pl.when(has_left)
@@ -411,23 +422,17 @@
         rhs_total = rhs_now if rhs_total is None else rhs_total + rhs_now
         tiled = jnp.concatenate([rhs_now] * NPAR + [jnp.zeros_like(rhs_now)], axis=0)
         normal = pick_left(same_source, tiled, NT)
-        moved = source_term(pick_right(gathered * normal, step_sel))
-        base = base - moved
-        resid = resid - jnp.where(live, moved, 0.0)
-
-        pulled = jnp.concatenate(
-            [att_partials[a].astype(F32) * resid for a in range(NAX)], axis=1
-        )
-        grads = full_dot(pulled, back)
+        step = pick_right(gathered * normal, step_sel)
+        grads_moved = jnp.zeros((cross, LANES), F32)
+        for q in range(NPAR):
+            grads_moved = grads_moved + step[:, q * rows : (q + 1) * rows] * cross_terms[q]
+        grads = grads_before - jnp.where(live_knots, grads_moved, 0.0)
         both = jnp.concatenate(
             [jnp.where(lane_low, grads, 0.0), jnp.where(lane_low, 0.0, grads)], axis=0
         )
         windows = pick_left(window_hot, both)
         grad_mine[it] = windows[: n_sky * span2].reshape(n_sky, span2, LANES)
         rim_mine[it] = windows[n_sky * span2 :].reshape(2, HALO, LANES)
-        for i in range(1, n_sky):
-            grad_copy(it, i).start()
-
         @pl.when(t < n_tm - 1)
         def _():
             low_copy(it, s).start()
@@ -436,8 +441,14 @@
         def _():
             high_copy(it, s).start()
 
+        for i in range(1, n_sky):
+            grad_copy(it, i).start()
+
         grad_all[it, s] = grad_mine[it, s]
 
+        if it < ITERS - 1:
+            base = base - source_term(step)
+            on_base = against_params(base)
         if it == ITERS - 1:
             full_hot = onehot(
                 iota((n_src, n_tm * cross), 0).astype(F32) == slots_all
@@ -484,9 +495,9 @@
             for b in range(n_band):
                 total = total + bands[b] * sums[:, b * LANES : (b + 1) * LANES]
             delta = total * inv_diag
-        knots_own = knots_own + delta[HALO : HALO + blocks]
+        knots_moved = knots_moved + delta[HALO : HALO + blocks]
         if it < ITERS - 1:
-            knots_all[it + 1, s] = pack(knots_own)
+            knots_all[it + 1, s] = pack(knots_own + knots_moved)
             for i in range(1, n_sky):
                 knots_copy(it + 1, i).start()
             for i in range(1, n_sky):
@@ -497,8 +508,8 @@
     own = (iota((blocks, knots_here), 1) >> 4) == iota((blocks, knots_here), 0)
     for a in range(NAX):
         unfold = onehot(jnp.logical_and((c >> 4) == a, (c & 15) == (d & 15)))
-        line = jnp.where(own, pick_right(knots_own, unfold), 0.0)
-        attitude_out[a] = jnp.sum(line, axis=0, keepdims=True)
+        line = jnp.where(own, pick_right(knots_moved, unfold), 0.0)
+        attitude_out[a] = attitude[a] + jnp.sum(line, axis=0, keepdims=True)
 
     for it in range(ITERS):
         for i in range(1, n_sky):

time: 43 us -> 39.3 us (0.914)
  Pallas kernels: 39.3 us -> 35.8 us
    pallas_call x1, Pallas kernels: 39.3 us -> 35.8 us  [per_device(): pl.pallas_call(functools.partial(kernel, n_sky, n_tm), out_shape=(jax.Sha...]
where the time goes in v2:
time: 39.3 us; the launch traced here: 39 us
  Pallas kernels  35.8 us (91%)
  local copies, waits for them, and re-layouts  1.98 us (5%)
  between operations  1.3 us (3%)
    pallas_call x1, Pallas kernels, per_device(): pl.pallas_call(functools.partial(kernel, n_sky, n_tm), out_shape=(jax.Sha...  35.8 us
    unnamed x4, local copies, waits for them, and re-layouts  1.98 us

profile of v2, /device:TPU:0, one launch (start us, length us, event | category | flops | bytes accessed | tf_op | source)
XLA Modules:
  0.0 39.0 jit_solution(7700582098480557033)
XLA Ops:
  1.3 35.8 %shard_map.131 = (f32[5,1024]{1,0:T(8,128)}, f32[3,1,512]{2,1,0:T(1,128)}) custom-call(f32[128,128]{1,0:T(8,128)} %observed.1, bf16[3,128,128]{2,1,0:T(8,128)(2,1)} %att_partials.1, bf16[5,128,128]{2,1,0:T(8,128)(2,1)} %src_partials.1, s32[1,128]{1,0:T(1,128)} %bitcast.2, s32[1,128]{1,0:T(1,128)} %bitcast.3, s32[1]{0:T(128)S(6)} %copy.16.live_count, ...), custom_call_target="tpu_custom_call" | custom-call | tf_op jit(solution)/shard_map/pallas_call | solution.py:558
  37.1 0.0 copy-start
  37.1 1.4 %copy.17 = f32[5,1024]{1,0:T(8,128)} copy(f32[5,1024]{1,0:T(8,128)} %get-tuple-element.4) | data formatting | bytes 40960
  38.4 0.0 copy-done
  38.5 0.6 %copy.18 = f32[3,1,512]{2,1,0:T(1,128)} copy(f32[3,1,512]{2,1,0:T(1,128)S(1)} %copy-done) | data formatting | bytes 12288
Async XLA Ops:
  37.1 1.4 %copy-start = (f32[3,1,512]{2,1,0:T(1,128)S(1)}, f32[3,1,512]{2,1,0:T(1,128)}, u32[]{:S(2)}) copy-start(f32[3,1,512]{2,1,0:T(1,128)} %get-tuple-element.5) | copy-start | bytes 18436

commit v3 on v2

--- a/solution.py
+++ b/solution.py
@@ -535,6 +535,11 @@
         edge_copy(1).wait_send()
 
 
+def finish(sources_in, attitude_in, sources_out, attitude_out):
+    sources_out[...] = sources_in[...]
+    attitude_out[...] = attitude_in[...]
+
+
 def per_device(
     observed,
     att_partials,
@@ -555,7 +560,7 @@
     vmem = pl.BlockSpec(memory_space=pltpu.VMEM)
     smem = pl.BlockSpec(memory_space=pltpu.SMEM)
     dma = pltpu.SemaphoreType.DMA
-    return pl.pallas_call(
+    results = pl.pallas_call(
         functools.partial(kernel, n_sky, n_tm),
         out_shape=(
             jax.ShapeDtypeStruct(sources.shape, F32),
@@ -600,6 +605,15 @@
         extra_diag,
         band_offsets,
     )
+    return pl.pallas_call(
+        finish,
+        out_shape=(
+            jax.ShapeDtypeStruct(sources.shape, F32),
+            jax.ShapeDtypeStruct(attitude.shape, F32),
+        ),
+        in_specs=[vmem] * 2,
+        out_specs=(vmem, vmem),
+    )(*results)
 
 
 def solution(mesh):

time: 39.3 us -> 38.7 us (0.985)
  local copies, waits for them, and re-layouts: 1.98 us -> 0 us
  Pallas kernels: 35.8 us -> 37.2 us
    unnamed x4 -> x0, local copies, waits for them, and re-layouts: 1.98 us -> none
    pallas_call x0 -> x1, Pallas kernels: none -> 1.38 us  [per_device(): pl.pallas_call(finish, out_shape=(jax.ShapeDtypeStruct(sources.shape, F32...]
where the time goes in v3:
time: 38.7 us; the launch traced here: 38.4 us
  Pallas kernels  37.2 us (96%)
  between operations  1.29 us (3%)
    pallas_call x1, Pallas kernels, per_device(): pl.pallas_call(functools.partial(kernel, n_sky, n_tm), out_shape=(jax.Sha...  35.8 us
    pallas_call x1, Pallas kernels, per_device(): pl.pallas_call(finish, out_shape=(jax.ShapeDtypeStruct(sources.shape, F32...  1.38 us

profile of v3, /device:TPU:0, one launch (start us, length us, event | category | flops | bytes accessed | tf_op | source)
XLA Modules:
  0.0 38.4 jit_solution(4484459537510054677)
XLA Ops:
  1.3 35.8 %shard_map.131 = (f32[5,1024]{1,0:T(8,128)}, f32[3,1,512]{2,1,0:T(1,128)}) custom-call(f32[128,128]{1,0:T(8,128)} %observed.1, bf16[3,128,128]{2,1,0:T(8,128)(2,1)} %att_partials.1, bf16[5,128,128]{2,1,0:T(8,128)(2,1)} %src_partials.1, s32[1,128]{1,0:T(1,128)} %bitcast.2, s32[1,128]{1,0:T(1,128)} %bitcast.3, s32[1]{0:T(128)S(6)} %copy.14.live_count, ...), custom_call_target="tpu_custom_call" | custom-call | tf_op jit(solution)/shard_map/pallas_call | solution.py:563
  37.1 1.4 %shard_map.132 = (f32[5,1024]{1,0:T(8,128)}, f32[3,1,512]{2,1,0:T(1,128)}) custom-call(f32[5,1024]{1,0:T(8,128)} %get-tuple-element.4.sources_in, f32[3,1,512]{2,1,0:T(1,128)} %get-tuple-element.5.attitude_in), custom_call_target="tpu_custom_call" | custom-call | tf_op jit(solution)/shard_map/pallas_call | solution.py:608
